TPU v7x, 256 devices: a whole 4x4x8 slice. The times are simulated.
256 devices in a mesh: lang: 4 (over x_hi, core), blk: 64 (over x_lo, z, y).
Axes of the slice: x: 4 (x_hi: 2, x_lo: 2; x = x_hi * 2 + x_lo), y: 4, z: 8, core: 2. Of those that a mesh axis runs over, the one named last changes fastest.
Arguments:
- fisher: bfloat16 [8, 4096, 16384], P('lang', None, 'blk'), may hold values from 0.049804688 to 5
- factor_left: bfloat16 [8, 4096, 64], P('lang', 'blk'), may hold values from -6 to 6
- factor_right: bfloat16 [8, 64, 16384], P('lang', None, 'blk'), may hold values from -0.75 to 0.75
- base_weight: bfloat16 [4096, 16384], P(('lang', 'blk')), may hold values from -3 to 3
Outputs:
- merged: bfloat16 [4096, 16384], P(('lang', 'blk'))
All inputs are finite; a program needn't handle non-finite values.
Results may differ from a plain program's by a relative error of at most 0.0011.
Values may be sent and summed in bfloat16 or wider, within the bound.
A program may use at most 128 MiB of HBM per device.

v0:
```python
import jax
import jax.numpy as jnp
from jax import lax
from jax.sharding import PartitionSpec as P


def weighted_sums(fisher_part, change):
    weight_wide = fisher_part.astype(jnp.float32)
    return (jnp.sum(weight_wide * change, axis=0), jnp.sum(weight_wide, axis=0))


def shards(fisher, factor_left, factor_right, base_weight):
    lang_count = lax.axis_size("lang")
    blk_count = lax.axis_size("blk")
    local_langs, full_rows, columns = fisher.shape
    row_count = base_weight.shape[0]
    change = jnp.einsum(
        "lir,lrc->lic",
        lax.all_gather(factor_left, "blk", axis=1, tiled=True),
        factor_right,
        preferred_element_type=jnp.float32,
    )
    weighted, totals = weighted_sums(fisher, change)
    weighted = weighted.reshape(lang_count, blk_count, row_count, columns)
    totals = totals.reshape(lang_count, blk_count, row_count, columns)
    moved = (
        lax.all_to_all(weighted, "blk", split_axis=1, concat_axis=3, tiled=True),
        lax.all_to_all(totals, "blk", split_axis=1, concat_axis=3, tiled=True),
    )
    weighted, totals = (
        lax.psum_scatter(moved[0], "lang", scatter_dimension=0, tiled=True),
        lax.psum_scatter(moved[1], "lang", scatter_dimension=0, tiled=True),
    )
    weighted = weighted.reshape(row_count, columns * blk_count)
    totals = totals.reshape(row_count, columns * blk_count)
    return (base_weight.astype(jnp.float32) + weighted / totals).astype(jnp.bfloat16)


def solution(mesh):
    placed = (
        P("lang", None, "blk"),
        P("lang", "blk", None),
        P("lang", None, "blk"),
        P(("lang", "blk"), None),
    )
    return jax.shard_map(
        shards, mesh=mesh, in_specs=placed, out_specs=P(("lang", "blk"), None), check_vma=False
    )
```

profile of v0, /device:TPU:32, one launch (start us, length us, event | category | flops | bytes accessed | tf_op | source)
XLA Modules:
  0.0 474.4 jit_solution(10156410915796598512)
XLA Ops:
  7.4 0.0 copy-start
  7.4 3.5 convert_reduce_fusion
  10.9 2.4 copy.9
  13.3 12.9 %all-to-all-start.1 = ((f32[4,64,16,256]{3,2,0,1:T(8,128)}), f32[4,64,16,256]{3,2,0,1:T(8,128)}, u32[]{:S(2)}, u32[]{:S(2)}) async-start(f32[4,64,16,256]{3,2,0,1:T(8,128)} %copy.9), calls=%async_computation.2 | async-start | bytes 8388608 | tf_op jit(solution)/shard_map/all_to_all | solution.py:28
  26.2 0.0 all-gather.2.cloned.1.call-start
  26.2 0.7 all-gather.2.cloned.1.call-update
  26.9 0.0 reduce-scatter.5.cloned.1.call-start
  27.0 93.8 %all-to-all-done.1 = f32[4,64,16,256]{3,2,0,1:T(8,128)} async-done(((f32[4,64,16,256]{3,2,0,1:T(8,128)}), f32[4,64,16,256]{3,2,0,1:T(8,128)}, u32[]{:S(2)}, u32[]{:S(2)}) %all-to-all-start.1) | async-done | bytes 4194336 | tf_op jit(solution)/shard_map/all_to_all | solution.py:28
  120.7 4.5 copy.12
  125.3 0.0 reduce-scatter.5.cloned.1.call-update
  125.3 0.0 reduce-scatter.3.cloned.1.call-start
  125.3 207.9 %all-gather.2.cloned.1.call-done = bf16[2,4096,64]{2,1,0:T(8,128)(2,1)} async-done(((bf16[2,64,64]{2,1,0:T(8,128)(2,1)}), bf16[2,4096,64]{2,1,0:T(8,128)(2,1)}) %all-gather.2.cloned.1.call-update) | async-done | bytes 1048592 | tf_op jit(solution)/shard_map/all_gather | solution.py:19
  333.3 0.0 copy-done
  333.3 4.4 fusion
  337.7 0.5 copy.7
  338.2 71.0 %all_to_all.36 = f32[4,64,16,256]{3,2,0,1:T(8,128)S(1)} all-to-all(f32[4,64,16,256]{3,2,0,1:T(8,128)S(1)} %copy.7), channel_id=1, replica_groups=mesh['lang'=4,'blk'=64] {'blk'}, dimensions={1} | all-to-all | bytes 8388608 | tf_op jit(solution)/shard_map/all_to_all | solution.py:27
  409.1 2.4 copy.11
  411.5 0.0 copy-start.1
  411.5 0.0 reduce-scatter.3.cloned.1.call-update
  411.5 0.0 reduce-scatter.5.cloned.1.call-done
  411.6 52.9 %reduce-scatter.3.cloned.1.call-done = f32[1,1,16,16384]{3,2,0,1:T(8,128)} async-done(((f32[4,1,16,16384]{3,2,0,1:T(8,128)}), f32[1,1,16,16384]{3,2,0,1:T(8,128)}) %reduce-scatter.3.cloned.1.call-update) | async-done | bytes 1048592 | tf_op jit(solution)/shard_map/reduce_scatter | solution.py:31
  464.5 0.0 copy-done.1
  464.5 2.5 fusion.1
Async XLA Ops:
  7.4 325.9 %copy-start = (bf16[2,64,256]{2,1,0:T(8,128)(2,1)S(1)}, bf16[2,64,256]{2,1,0:T(8,128)(2,1)}, u32[]{:S(2)}) copy-start(bf16[2,64,256]{2,1,0:T(8,128)(2,1)} %param.6) | copy-start | bytes 196612
  13.3 107.4 %all-to-all-start.1 = ((f32[4,64,16,256]{3,2,0,1:T(8,128)}), f32[4,64,16,256]{3,2,0,1:T(8,128)}, u32[]{:S(2)}, u32[]{:S(2)}) async-start(f32[4,64,16,256]{3,2,0,1:T(8,128)} %copy.9), calls=%async_computation.2 | async-start | bytes 8388608 | tf_op jit(solution)/shard_map/all_to_all | solution.py:28
  26.2 307.1 %all-gather.2.cloned.1.call-start = ((), (), s32[]{:S(2)}) async-start(), calls=%async_computation.4 | async-start | bytes 2129920 | tf_op jit(solution)/shard_map/all_gather | solution.py:19
  26.9 384.7 %reduce-scatter.5.cloned.1.call-start = ((), (), s32[]{:S(2)}) async-start(), calls=%async_computation.6 | async-start | bytes 5242880 | tf_op jit(solution)/shard_map/reduce_scatter | solution.py:32
  125.3 339.2 %reduce-scatter.3.cloned.1.call-start = ((), (), s32[]{:S(2)}) async-start(), calls=%async_computation.5 | async-start | bytes 5242880 | tf_op jit(solution)/shard_map/reduce_scatter | solution.py:31
  411.5 53.0 %copy-start.1 = (bf16[16,16384]{1,0:T(8,128)(2,1)S(1)}, bf16[16,16384]{1,0:T(8,128)(2,1)}, u32[]{:S(2)}) copy-start(bf16[16,16384]{1,0:T(8,128)(2,1)} %param.7) | copy-start | bytes 1572868
Sparse Core Ops, SparseCore 0:
  28.9 304.3 all-gather.1
Sparse Core Ops, SparseCore 1:
  125.4 60.8 reduce-scatter.4
  411.6 52.8 reduce-scatter.2
where the time goes:
time: 476 us; the launch traced here: 474 us
  waiting for transfers between devices  355 us (75%)
  blocking collectives  71 us (15%)
  between operations  14.9 us (3%)
  starting transfers between devices  13 us (3%)
  local copies, waits for them, and re-layouts  9.77 us (2%)
  other arithmetic  6 us (1%)
    all_gather x1, waiting for transfers between devices, shards(): lax.all_gather(factor_left, 'blk', axis=1, tiled=True)  208 us
    all_to_all x1, waiting for transfers between devices, shards(): lax.all_to_all(totals, 'blk', split_axis=1, concat_axis=3, tiled=True)  93.8 us
    all_to_all x1, blocking collectives, shards(): lax.all_to_all(weighted, 'blk', split_axis=1, concat_axis=3, tiled=True)  71 us
    reduce_scatter x1, waiting for transfers between devices, shards(): lax.psum_scatter(moved[0], 'lang', scatter_dimension=0, tiled=True)  52.9 us
    all_to_all x1, starting transfers between devices, shards(): lax.all_to_all(totals, 'blk', split_axis=1, concat_axis=3, tiled=True)  12.9 us
  transfers between devices with their start and end apart: 4, of which 3 were waited for; matrix products, arithmetic and copies ran while one was open for 2% of the time, Pallas kernels for 0%

commit v1 on v0

v1 whole, which is shorter than its diff:
```python
import jax
import jax.numpy as jnp
from jax import lax
from jax.experimental import pallas as pl
from jax.experimental.pallas import tpu as pltpu
from jax.sharding import PartitionSpec as P

BF16, F32 = jnp.bfloat16, jnp.float32
NZ, NY = 8, 4
LAG = 3
W_KNEE, W_SCALE = 0.25, 2.0**-7.25
D_KNEE, D_SCALE = 0.01, 2.0**-7.4


def encode(v, knee, scale):
    c = jnp.abs(v) * (scale / knee) + scale
    c = c * c
    c = c * c
    c = c * c
    c = c * c
    return jnp.where(v < 0, -c, c).astype(BF16)


def root16(y):
    return jnp.exp2(jnp.log2(y) * (1.0 / 16))


def decode(y, knee, scale):
    y = y.astype(F32)
    v = root16(jnp.abs(y)) * (knee / scale) - knee
    return jnp.where(y < 0, -v, v)


def encode_total(t):
    c = t * 0.5
    c = c * c
    c = c * c
    c = c * c
    return (c * c).astype(BF16)


def decode_total(y):
    return root16(y.astype(F32)) * 2.0


def kernel(fisher, left, right, base, out, packed, lefts, rights, weights, fish, sent, own, got, delta_out, delta_in,
           f_local, f_send, f_recv, r_sem, l_send, l_first, l_recv, y_send, y_recv, x_send, x_recv, d_send, d_recv):
    lang, blk = lax.axis_index("lang"), lax.axis_index("blk")
    xh, core = lang // 2, lang % 2
    xl, z, y = blk // 32, (blk // 4) % 8, blk % 4
    x = 2 * xh + xl
    zc = z // 4
    other = 1 - core

    def dev(xh_, c_, xl_, z_, y_):
        return {"lang": 2 * xh_ + c_, "blk": 32 * xl_ + 4 * z_ + y_}

    def remote(src, dst, send, recv, device):
        return pltpu.make_async_remote_copy(
            src_ref=src, dst_ref=dst, send_sem=send, recv_sem=recv, device_id=device, device_id_type=pl.DeviceIdType.MESH
        )

    barrier = pltpu.get_barrier_semaphore()

    def greet(device):
        pl.semaphore_signal(barrier, inc=1, device_id=device, device_id_type=pl.DeviceIdType.MESH)

    greet(dev(1 - xh, core, xl, z, y))
    greet(dev(1 - xh, core, 1 - xl, z, y))
    greet(dev(xh, other, xl, z, y))

    def greet_line(k, carry):
        greet(dev(xh, (core + k // 16) % 2, (xl + (k // 8) % 2) % 2, (z + k) % 8, y))
        return carry

    lax.fori_loop(1, 16, greet_line, 0)
    lax.fori_loop(17, 32, greet_line, 0)

    def greet_plane(k, carry):
        greet(dev(xh, core, xl, (z + k) % 8, (y + 1 + k // 8) % 4))
        return carry

    lax.fori_loop(0, 24, greet_plane, 0)

    def rows(g, c_):
        return pl.ds(pl.multiple_of(1024 * (2 * (g // 2) + c_) + 512 * (g % 2), 512), 512)

    local = [pltpu.make_async_copy(fisher.at[:, rows(g, core), :], fish.at[g, core], f_local.at[g]) for g in range(4)]
    for copy in local:
        copy.start()
    r_local = pltpu.make_async_copy(right, rights.at[core], r_sem.at[0])
    r_local.start()
    packed[...] = jnp.concatenate([left[0], left[1]], axis=1)
    weights[...] = jnp.zeros_like(weights)
    pl.semaphore_wait(barrier, 57)

    g_own = 2 * xl + (z // 2) % 2
    zb_own = z % 2
    slot = lefts.at[g_own, zb_own * 4 + y, core]
    slot_sem = l_recv.at[g_own * 2 + zb_own, core]
    first_local = pltpu.make_async_copy(packed, slot, slot_sem)
    first_remote = remote(packed, slot, l_first, slot_sem, dev(xh, zc, xl, z, y))

    @pl.when(zc == core)
    def _():
        first_local.start()

    @pl.when(zc != core)
    def _():
        first_remote.start()

    def left_copy(k):
        return remote(packed, slot, l_send.at[k], slot_sem, dev(xh, zc, (xl + k // 8) % 2, (z + k) % 8, y))

    def left_start(k, carry):
        left_copy(k).start()
        return carry

    lax.fori_loop(1, 16, left_start, 0)

    r_remote = remote(right, rights.at[core], r_sem.at[1], r_sem.at[2], dev(xh, other, xl, z, y))
    r_remote.start()
    f_remote = [
        remote(fisher.at[:, rows(g, other), :], fish.at[g, core], f_send.at[g], f_recv.at[g], dev(xh, other, xl, z, y))
        for g in range(4)
    ]
    for copy in f_remote:
        copy.start()
    r_local.wait()
    r_remote.wait_recv()
    for s in range(2):
        for i in range(2):
            weights[s, 64 * i : 64 * i + 64, 256 * i : 256 * i + 256] = rights[s, i]
    for g in range(4):
        local[g].wait()
        f_remote[g].wait_recv()

    def left_pass(g, u, k):
        return remote(lefts.at[g, u], lefts.at[g, u], y_send.at[g * 2 + u // 4, k - 1], y_recv.at[g, u],
                      dev(xh, core, xl, z, (y + k) % 4))

    def unit_of(step):
        k = step // 2
        ys = (y + k + (k // 2) * (1 - 2 * (k % 2))) % 4
        return (step % 2) * 4 + ys

    def partial(g, u):
        at = pl.ds(pl.multiple_of(u * 64, 64), 64)
        w = t = None
        for s in range(2):
            change = jnp.dot(lefts[g, u, s], weights[s], preferred_element_type=F32)
            for i in range(2):
                f = fish[g, s, i, at, :].astype(F32)
                term = f * change[:, 256 * i : 256 * i + 256]
                w = term if w is None else w + term
                t = f if t is None else t + f
        return w, t

    def x_copy(rel, u):
        target = (x + rel) % 4
        return remote(sent.at[rel - 1, u], got.at[rel - 1, u], x_send.at[rel - 1, u], x_recv.at[rel - 1, u],
                      dev(target // 2, core, target % 2, z, y))

    def compute(step):
        u = unit_of(step)
        for rel in (2, 1, 3, 0):
            g = (x + rel) % 4

            @pl.when(step < 2)
            def _():
                for s in range(2):
                    pltpu.make_async_copy(packed, lefts.at[g, u, s], l_recv.at[g * 2 + u // 4, s]).wait()
                for k in (2, 1, 3):
                    left_pass(g, u, k).start()

            @pl.when(step >= 2)
            def _():
                left_pass(g, u, 1).wait_recv()

            w, t = partial(g, u)
            if rel:
                sent[rel - 1, u, 0] = encode(w, W_KNEE, W_SCALE)
                sent[rel - 1, u, 1] = encode_total(t)
                x_copy(rel, u).start()
            else:
                own[u, 0] = w
                own[u, 1] = t

    def d_copy(u, k):
        return remote(delta_out.at[u, k], delta_in.at[z * 4 + y], d_send.at[u, k], d_recv.at[z * 4 + y],
                      dev(xh, core, xl, u, k))

    self_copy = pltpu.make_async_copy(delta_out.at[z, y], delta_in.at[z * 4 + y], d_recv.at[z * 4 + y])

    def combine(step):
        u = unit_of(step)
        for rel in (1, 2, 3):
            x_copy(rel, u).wait_recv()
        w = own[u, 0] + decode(got[1, u, 0], W_KNEE, W_SCALE)
        t = own[u, 1] + decode_total(got[1, u, 1])
        near = encode(w / t, D_KNEE, D_SCALE)
        w = decode(got[0, u, 0], W_KNEE, W_SCALE) + decode(got[2, u, 0], W_KNEE, W_SCALE)
        t = decode_total(got[0, u, 1]) + decode_total(got[2, u, 1])
        far = encode(w / t, D_KNEE, D_SCALE)
        for k in range(4):
            delta_out[u, k, :, :256] = near[16 * k : 16 * k + 16]
            delta_out[u, k, :, 256:] = far[16 * k : 16 * k + 16]
        for k in range(4):
            here = jnp.logical_and(u == z, k == y)

            @pl.when(here)
            def _():
                self_copy.start()

            @pl.when(jnp.logical_not(here))
            def _():
                d_copy(u, k).start()

    def step_body(step, carry):
        @pl.when(step < 8)
        def _():
            compute(step)

        @pl.when(step >= LAG)
        def _():
            combine(step - LAG)

        return carry

    lax.fori_loop(0, 8 + LAG, step_body, 0)

    def finish(n, carry):
        src = (z * 4 + y + n) % 32
        pltpu.make_async_copy(delta_out.at[0, 0], delta_in.at[src], d_recv.at[src]).wait()
        for part, half in ((0, xl), (1, 1 - xl)):
            at = pl.ds(pl.multiple_of((half * 32 + src) * 256, 256), 256)
            delta = decode(delta_in[src, :, 256 * part : 256 * part + 256], D_KNEE, D_SCALE)
            out[:, at] = (base[:, at].astype(F32) + delta).astype(BF16)
        return carry

    lax.fori_loop(0, 32, finish, 0)

    @pl.when(zc != core)
    def _():
        first_remote.wait_send()

    def left_sent(k, carry):
        left_copy(k).wait_send()
        return carry

    lax.fori_loop(1, 16, left_sent, 0)
    r_remote.wait_send()
    for copy in f_remote:
        copy.wait_send()

    def sent_all(u, carry):
        for rel in (1, 2, 3):
            x_copy(rel, u).wait_send()
        for k in range(4):
            @pl.when(jnp.logical_not(jnp.logical_and(u == z, k == y)))
            def _():
                d_copy(u, k).wait_send()
        return carry

    lax.fori_loop(0, 8, sent_all, 0)

    def passed_all(n, carry):
        for k in (1, 2, 3):
            left_pass(n // 2, (n % 2) * 4 + y, k).wait_send()
        return carry

    lax.fori_loop(0, 8, passed_all, 0)


def shards(fisher, factor_left, factor_right, base_weight):
    dma = pltpu.SemaphoreType.DMA
    hbm, vmem = pl.BlockSpec(memory_space=pl.ANY), pl.BlockSpec(memory_space=pltpu.VMEM)
    return pl.pallas_call(
        kernel,
        out_shape=jax.ShapeDtypeStruct(base_weight.shape, BF16),
        in_specs=[hbm, vmem, vmem, vmem],
        out_specs=vmem,
        scratch_shapes=[
            pltpu.VMEM((64, 128), BF16),
            pltpu.VMEM((4, 8, 2, 64, 128), BF16),
            pltpu.VMEM((2, 2, 64, 256), BF16),
            pltpu.VMEM((2, 128, 512), BF16),
            pltpu.VMEM((4, 2, 2, 512, 256), BF16),
            pltpu.VMEM((3, 8, 2, 64, 256), BF16),
            pltpu.VMEM((8, 2, 64, 256), F32),
            pltpu.VMEM((3, 8, 2, 64, 256), BF16),
            pltpu.VMEM((8, 4, 16, 512), BF16),
            pltpu.VMEM((32, 16, 512), BF16),
            dma((4,)),
            dma((4,)),
            dma((4,)),
            dma((3,)),
            dma((16,)),
            dma(()),
            dma((8, 2)),
            dma((8, 3)),
            dma((4, 8)),
            dma((3, 8)),
            dma((3, 8)),
            dma((8, 4)),
            dma((32,)),
        ],
        compiler_params=pltpu.CompilerParams(collective_id=0, has_side_effects=True, vmem_limit_bytes=48 * 2**20),
    )(fisher, factor_left, factor_right, base_weight)


def solution(mesh):
    placed = (
        P("lang", None, "blk"),
        P("lang", "blk", None),
        P("lang", None, "blk"),
        P(("lang", "blk"), None),
    )
    return jax.shard_map(
        shards, mesh=mesh, in_specs=placed, out_specs=P(("lang", "blk"), None), check_vma=False
    )
```

time: 476 us -> 58.4 us (0.12)
  waiting for transfers between devices: 355 us -> 0 us
  blocking collectives: 71 us -> 0 us
  Pallas kernels: 0 us -> 52.5 us
  between operations: 14.9 us -> 0.01 us
  starting transfers between devices: 13 us -> 0 us
  other arithmetic: 6 us -> 0 us
    all_gather x1 -> x0, waiting for transfers between devices: 208 us -> none  [shards(): lax.all_gather(factor_left, 'blk', axis=1, tiled=True)]
    all_to_all x1 -> x0, waiting for transfers between devices: 93.8 us -> none  [shards(): lax.all_to_all(totals, 'blk', split_axis=1, concat_axis=3, tiled=True)]
    all_to_all x1 -> x0, blocking collectives: 71 us -> none  [shards(): lax.all_to_all(weighted, 'blk', split_axis=1, concat_axis=3, tiled=True)]
    reduce_scatter x2 -> x0, waiting for transfers between devices: 53 us -> none  [the longest x1 52.9 us: shards(): lax.psum_scatter(moved[0], 'lang', scatter_dimension=0, tiled=True)]
    pallas_call x0 -> x1, Pallas kernels: none -> 52.5 us  [shards(): pl.pallas_call(kernel, out_shape=jax.ShapeDtypeStruct(base_weight.shape,...]
    all_to_all x1 -> x0, starting transfers between devices: 12.9 us -> none  [shards(): lax.all_to_all(totals, 'blk', split_axis=1, concat_axis=3, tiled=True)]
    all_to_all x2 -> x0, local copies, waits for them, and re-layouts: 6.9 us -> none  [the longest x1 4.54 us: shards(): lax.all_to_all(totals, 'blk', split_axis=1, concat_axis=3, tiled=True)]
    unnamed x4 -> x9, local copies, waits for them, and re-layouts: 0.01 us -> 5.62 us
  transfers between devices with their start and end apart: 4 -> 0, of which waited for: 3 -> 0; matrix products, arithmetic and copies ran while one was open for 2% -> 0% of each run, Pallas kernels for 0% -> 0%
where the time goes in v1:
time: 58.4 us; the launch traced here: 58.1 us
  Pallas kernels  52.5 us (90%)
  local copies, waits for them, and re-layouts  5.62 us (10%)
    pallas_call x1, Pallas kernels, shards(): pl.pallas_call(kernel, out_shape=jax.ShapeDtypeStruct(base_weight.shape,...  52.5 us
    unnamed x9, local copies, waits for them, and re-layouts  5.62 us

profile of v1, /device:TPU:32, one launch (start us, length us, event | category | flops | bytes accessed | tf_op | source)
XLA Modules:
  0.0 58.1 jit_solution(3119512828321891355)
XLA Ops:
  0.0 0.0 copy-start
  0.0 2.2 %copy-done = bf16[2,4096,256]{2,1,0:T(8,128)(2,1)S(1)} copy-done((bf16[2,4096,256]{2,1,0:T(8,128)(2,1)S(1)}, bf16[2,4096,256]{2,1,0:T(8,128)(2,1)}, u32[]{:S(2)}) %copy-start) | copy-done | bytes 4194328
  2.2 0.0 copy-start.1
  2.2 1.0 %copy-done.1 = bf16[16,16384]{1,0:T(8,128)(2,1)S(1)} copy-done((bf16[16,16384]{1,0:T(8,128)(2,1)S(1)}, bf16[16,16384]{1,0:T(8,128)(2,1)}, u32[]{:S(2)}) %copy-start.1) | copy-done | bytes 524312
  3.2 0.0 copy-start.2
  3.2 0.8 %copy-done.2 = bf16[2,64,256]{2,1,0:T(8,128)(2,1)S(1)} copy-done((bf16[2,64,256]{2,1,0:T(8,128)(2,1)S(1)}, bf16[2,64,256]{2,1,0:T(8,128)(2,1)}, u32[]{:S(2)}) %copy-start.2) | copy-done | bytes 65560
  4.1 0.0 copy-start.3
  4.1 0.8 %copy-done.3 = bf16[2,64,64]{2,1,0:T(8,128)(2,1)S(1)} copy-done((bf16[2,64,64]{2,1,0:T(8,128)(2,1)S(1)}, bf16[2,64,64]{2,1,0:T(8,128)(2,1)}, u32[]{:S(2)}) %copy-start.3) | copy-done | bytes 16408
  4.8 52.5 %shard_map.46 = bf16[16,16384]{1,0:T(8,128)(2,1)S(1)} custom-call(bf16[2,4096,256]{2,1,0:T(8,128)(2,1)S(1)} %copy-done, bf16[2,64,64]{2,1,0:T(8,128)(2,1)S(1)} %copy-done.3, bf16[2,64,256]{2,1,0:T(8,128)(2,1)S(1)} %copy-done.2, bf16[16,16384]{1,0:T(8,128)(2,1)S(1)} %copy-done.1), custom_call_target="tpu_custom_call" | custom-call | tf_op jit(solution)/shard_map/pallas_call | solution.py:278
  57.3 0.8 %copy.6 = bf16[16,16384]{1,0:T(8,128)(2,1)} copy(bf16[16,16384]{1,0:T(8,128)(2,1)S(1)} %shard_map.46) | data formatting | bytes 1048576
Async XLA Ops:
  0.0 2.2 %copy-start = (bf16[2,4096,256]{2,1,0:T(8,128)(2,1)S(1)}, bf16[2,4096,256]{2,1,0:T(8,128)(2,1)}, u32[]{:S(2)}) copy-start(bf16[2,4096,256]{2,1,0:T(8,128)(2,1)} %fisher.1) | copy-start | bytes 12582916
  2.2 1.0 %copy-start.1 = (bf16[16,16384]{1,0:T(8,128)(2,1)S(1)}, bf16[16,16384]{1,0:T(8,128)(2,1)}, u32[]{:S(2)}) copy-start(bf16[16,16384]{1,0:T(8,128)(2,1)} %base.1) | copy-start | bytes 1572868
  3.2 0.8 %copy-start.2 = (bf16[2,64,256]{2,1,0:T(8,128)(2,1)S(1)}, bf16[2,64,256]{2,1,0:T(8,128)(2,1)}, u32[]{:S(2)}) copy-start(bf16[2,64,256]{2,1,0:T(8,128)(2,1)} %right.1) | copy-start | bytes 196612
  4.1 0.8 %copy-start.3 = (bf16[2,64,64]{2,1,0:T(8,128)(2,1)S(1)}, bf16[2,64,64]{2,1,0:T(8,128)(2,1)}, u32[]{:S(2)}) copy-start(bf16[2,64,64]{2,1,0:T(8,128)(2,1)} %left.1) | copy-start | bytes 49156

commit v2 on v0

v2 whole, which is shorter than its diff:
```python
import jax
import jax.numpy as jnp
from jax import lax
from jax.experimental import pallas as pl
from jax.experimental.pallas import tpu as pltpu
from jax.sharding import PartitionSpec as P

BF16, F32 = jnp.bfloat16, jnp.float32
NZ, NY = 8, 4
MESH = pl.DeviceIdType.MESH
LAG = 3
W_KNEE, W_SCALE = 0.25, 2.0**-7.25
D_KNEE, D_SCALE = 0.01, 2.0**-7.4


def encode(v, knee, scale):
    c = jnp.abs(v) * (scale / knee) + scale
    c = c * c
    c = c * c
    c = c * c
    c = c * c
    return jnp.where(v < 0, -c, c).astype(BF16)


def root16(y):
    return jnp.exp2(jnp.log2(y) * (1.0 / 16))


def decode(y, knee, scale):
    y = y.astype(F32)
    v = root16(jnp.abs(y)) * (knee / scale) - knee
    return jnp.where(y < 0, -v, v)


def encode_total(t):
    c = t * 0.5
    c = c * c
    c = c * c
    c = c * c
    return (c * c).astype(BF16)


def decode_total(y):
    return root16(y.astype(F32)) * 2.0


def kernel(fisher, left_hbm, right, base_hbm, out, left, base, packed, lefts, rights, weights, fish, t_sent, t_own, t_got,
           w_sent, w_own, w_got, delta_out, delta_in, in_sem, f_local, f_send, f_recv, r_sem, p_send, p_recv, z_send, y_send, l_recv,
           t_send, t_recv, w_send, w_recv, d_send, d_recv, token):
    lang, blk = lax.axis_index("lang"), lax.axis_index("blk")
    xh, core = lang // 2, lang % 2
    xl, z, y = blk // 32, (blk // 4) % 8, blk % 4
    x = 2 * xh + xl
    zc, zi = z // 4, z % 4
    other = 1 - core

    def dev(xh_, c_, xl_, z_, y_):
        return {"lang": 2 * xh_ + c_, "blk": 32 * xl_ + 4 * z_ + y_}

    def remote(src, dst, send, recv, device):
        return pltpu.make_async_remote_copy(
            src_ref=src, dst_ref=dst, send_sem=send, recv_sem=recv, device_id=device, device_id_type=MESH
        )

    def signal(semaphore, device):
        pl.semaphore_signal(semaphore, inc=1, device_id=device, device_id_type=MESH)

    def in_z(n):
        return dev(xh, core, xl, (z + n) % 8, y)

    def in_y(n):
        return dev(xh, core, xl, z, (y + n) % 4)

    partner, beside = dev(xh, other, xl, z, y), dev(xh, core, 1 - xl, z, y)
    barrier = pltpu.get_barrier_semaphore()
    for device in (in_z(2), in_z(6), in_y(2), in_z(1), in_z(7), in_y(1), in_y(3), dev(1 - xh, core, xl, z, y),
                   dev(1 - xh, core, 1 - xl, z, y), beside, partner):
        signal(barrier, device)

    left_in = pltpu.make_async_copy(left_hbm, left, in_sem.at[0])
    left_in.start()

    def ranking(c):
        near, far = (228, 225, 54, 27), (27, 75, 180, 228)

        def pick(options):
            return jnp.where(zi < 2, jnp.where(zi == 0, options[0], options[1]), jnp.where(zi == 2, options[2], options[3]))

        return jnp.where(zc == c, pick(near), pick(far))

    rank, rank_other = ranking(core), ranking(other)

    def digit(word, n):
        return lax.shift_right_logical(word, 2 * n) & 3

    def rows(xs, c, zq):
        return pl.ds(pl.multiple_of(1024 * (2 * xs + c) + 256 * zq, 256), 256)

    def f_own(zq, xs):
        return pltpu.make_async_copy(fisher.at[:, rows(xs, core, zq), :], fish.at[zq, xs, core], f_local.at[zq, xs])

    def f_swap(zq, xs):
        return remote(fisher.at[:, rows(xs, other, zq), :], fish.at[zq, xs, core], f_send.at[zq, xs], f_recv.at[zq, xs], partner)

    for n in range(4):
        for xs in range(2):
            f_own(digit(rank, n), xs).start()
    r_local = pltpu.make_async_copy(right, rights.at[core], r_sem.at[0])
    r_local.start()
    base_in = pltpu.make_async_copy(base_hbm, base, in_sem.at[1])
    base_in.start()
    weights[...] = jnp.zeros_like(weights)
    left_in.wait()
    packed[...] = jnp.concatenate([left[0], left[1]], axis=1)
    pl.semaphore_wait(barrier, 11)

    signal(token.at[0], in_z(2))
    signal(token.at[0], in_z(6))
    home = zc == core
    p_local = pltpu.make_async_copy(packed, lefts.at[zi, y, core, xl], p_recv)
    p_near = remote(packed, lefts.at[zi, y, core, xl], p_send, p_recv, partner)

    @pl.when(home)
    def _():
        p_local.start()

    @pl.when(jnp.logical_not(home))
    def _():
        p_near.start()

    f_swap(digit(rank_other, 0), 0).start()
    f_swap(digit(rank_other, 0), 1).start()
    r_remote = remote(right, rights.at[core], r_sem.at[1], r_sem.at[2], partner)
    r_remote.start()
    for n in range(1, 4):
        for xs in range(2):
            f_swap(digit(rank_other, n), xs).start()

    def t_copy(g, zb):
        return remote(t_sent.at[g, zb], t_got.at[zb, (g - x + 4) % 4 - 1], t_send, t_recv, dev(g // 2, core, g % 2, z, y))

    def w_copy(g, u):
        return remote(w_sent.at[g, u], w_got.at[u, (g - x + 4) % 4 - 1], w_send, w_recv.at[u], dev(g // 2, core, g % 2, z, y))

    def totals(n, carry):
        zq, xs = digit(rank, n // 2), n % 2
        f_own(zq, xs).wait()
        pltpu.make_async_copy(fisher.at[:, rows(xs, core, zq), :], fish.at[zq, xs, other], f_recv.at[zq, xs]).wait()
        t = fish[zq, xs, 0, 0].astype(F32) + fish[zq, xs, 0, 1].astype(F32)
        t = t + (fish[zq, xs, 1, 0].astype(F32) + fish[zq, xs, 1, 1].astype(F32))
        g, zb = 2 * xs + zq // 2, zq % 2

        @pl.when(g == x)
        def _():
            t_own[zb] = t

        @pl.when(g != x)
        def _():
            t_sent[g, zb] = encode_total(t)
            t_copy(g, zb).start()

        return carry

    def spread(n, carry):
        to = dev(xh, core, (xl + n // 8) % 2, (z + n) % 8, y)
        remote(lefts.at[zi, y, :, xl], lefts.at[zi, y, :, xl], z_send, l_recv.at[zi, y], to).start()
        return carry

    lax.fori_loop(0, 2, totals, 0)
    pl.semaphore_wait(token.at[0], 2)
    signal(token.at[1], beside)

    @pl.when(home)
    def _():
        pltpu.make_async_copy(lefts.at[zi, y, :, xl], lefts.at[zi, y, :, xl], p_recv).wait()
        lax.fori_loop(1, 8, spread, 0)

    lax.fori_loop(2, 4, totals, 0)
    pl.semaphore_wait(token.at[1], 1)

    @pl.when(home)
    def _():
        lax.fori_loop(8, 16, spread, 0)

    lax.fori_loop(4, 8, totals, 0)
    r_local.wait()
    r_remote.wait_recv()
    for s in range(2):
        for i in range(2):
            weights[s, 64 * i : 64 * i + 64, 256 * i : 256 * i + 256] = rights[s, i]

    def pass_y(zq, n):
        return remote(lefts.at[zq, y], lefts.at[zq, y], y_send, l_recv.at[zq, y], in_y(n))

    def offset(k):
        return ((k + 1) % 3 + 1) * ((k + 2) // 3)

    def first_zb(ys):
        ahead = (ys - z + 8) % 8
        return jnp.where((ahead >= 2) & (ahead <= 5), 0, 1)

    def forward(n, carry):
        zq = n % 2 * 2 + (first_zb(y) + n // 2) % 2
        mine = home & (zq == zi)

        @pl.when(mine)
        def _():
            pltpu.make_async_copy(lefts.at[zq, y, :, 0], lefts.at[zq, y, :, 0], l_recv.at[zq, y]).wait()

        @pl.when(jnp.logical_not(mine))
        def _():
            pltpu.make_async_copy(lefts.at[zq, y], lefts.at[zq, y], l_recv.at[zq, y]).wait()

        pass_y(zq, 1).start()
        pass_y(zq, 3).start()
        pass_y(zq, 2).start()
        return carry

    lax.fori_loop(0, 4, forward, 0)

    def item(n, carry):
        k = n // 2 % 4
        ys = (y + offset(k)) % 4
        zq = n % 2 * 2 + (first_zb(ys) + n // 8) % 2

        @pl.when(k > 0)
        def _():
            pltpu.make_async_copy(lefts.at[zq, ys], lefts.at[zq, ys], l_recv.at[zq, ys]).wait()

        at = pl.ds(pl.multiple_of(ys * 64, 64), 64)
        u = (zq % 2) * 4 + ys
        w = None
        for s in range(2):
            lhs = lefts[zq, ys, s].reshape(128, 128)
            for i in range(2):
                change = jnp.dot(lhs, weights[s, :, 256 * i : 256 * i + 256], preferred_element_type=F32)
                term = fish[zq, :, s, i, at, :].astype(F32).reshape(128, 256) * change
                w = term if w is None else w + term
        for xs in range(2):
            g = 2 * xs + zq // 2
            half = slice(64 * xs, 64 * xs + 64)

            @pl.when(g == x)
            def _():
                w_own[u] = w[half]

            @pl.when(g != x)
            def _():
                w_sent[g, u] = encode(w[half], W_KNEE, W_SCALE)
                w_copy(g, u).start()

        return carry

    def combine(step, carry):
        ys = (y + offset(step % 4)) % 4
        zb = (first_zb(ys) + step // 4) % 2
        u = zb * 4 + ys

        @pl.when(step == 0)
        def _():
            pltpu.make_async_copy(t_got, t_got, t_recv).wait()

        pltpu.make_async_copy(w_got.at[u], w_got.at[u], w_recv.at[u]).wait()
        at = pl.ds(pl.multiple_of(ys * 64, 64), 64)
        w = w_own[u] + decode(w_got[u, 1], W_KNEE, W_SCALE)
        t = t_own[zb, at] + decode_total(t_got[zb, 1, at])
        near = encode(w / t, D_KNEE, D_SCALE)
        w = decode(w_got[u, 0], W_KNEE, W_SCALE) + decode(w_got[u, 2], W_KNEE, W_SCALE)
        t = decode_total(t_got[zb, 0, at]) + decode_total(t_got[zb, 2, at])
        far = encode(w / t, D_KNEE, D_SCALE)
        for k in range(4):
            delta_out[u, k, :, :256] = near[16 * k : 16 * k + 16]
            delta_out[u, k, :, 256:] = far[16 * k : 16 * k + 16]
        for k in range(4):
            here = jnp.logical_and(u == z, k == y)
            d_copy = remote(delta_out.at[u, k], delta_in.at[z * 4 + y], d_send, d_recv.at[z * 4 + y], dev(xh, core, xl, u, k))

            @pl.when(here)
            def _():
                pltpu.make_async_copy(delta_out.at[u, k], delta_in.at[z * 4 + y], d_recv.at[z * 4 + y]).start()

            @pl.when(jnp.logical_not(here))
            def _():
                d_copy.start()

        return carry

    def finish(n, carry):
        zs = (z + 3 + n % 4 + 4 * (n // 16)) % 8
        src = zs * 4 + (zi - offset(n // 4 % 4) + 4) % 4
        pltpu.make_async_copy(delta_out.at[0, 0], delta_in.at[src], d_recv.at[src]).wait()
        for part, half in ((0, xl), (1, 1 - xl)):
            at = pl.ds(pl.multiple_of((half * 32 + src) * 256, 256), 256)
            delta = decode(delta_in[src, :, 256 * part : 256 * part + 256], D_KNEE, D_SCALE)
            out[:, at] = (base[:, at].astype(F32) + delta).astype(BF16)
        return carry

    def unit(m, carry):
        @pl.when(m < 8)
        def _():
            lax.fori_loop(2 * m, 2 * m + 2, item, 0)

        @pl.when(m >= LAG)
        def _():
            combine(m - LAG, 0)

        return carry

    lax.fori_loop(0, 6 + LAG, unit, 0)
    base_in.wait()
    lax.fori_loop(0, 12, finish, 0)
    lax.fori_loop(6 + LAG, 8 + LAG, unit, 0)
    lax.fori_loop(12, 32, finish, 0)

    @pl.when(home)
    def _():
        pltpu.make_async_copy(delta_in.at[0:30], delta_in.at[0:30], z_send).wait()

    @pl.when(jnp.logical_not(home))
    def _():
        p_near.wait_send()

    r_remote.wait_send()
    for zq in range(4):
        for xs in range(2):
            f_swap(zq, xs).wait_send()
    for sem, view in ((y_send, lefts.at[0:3]), (t_send, t_got), (w_send, w_got), (d_send, delta_in.at[0:31])):
        pltpu.make_async_copy(view, view, sem).wait()


def shards(fisher, factor_left, factor_right, base_weight):
    dma = pltpu.SemaphoreType.DMA
    hbm, vmem = pl.BlockSpec(memory_space=pltpu.HBM), pl.BlockSpec(memory_space=pltpu.VMEM)
    return pl.pallas_call(
        kernel,
        out_shape=jax.ShapeDtypeStruct(base_weight.shape, BF16),
        in_specs=[hbm] * 4,
        out_specs=vmem,
        scratch_shapes=[
            pltpu.VMEM(factor_left.shape, BF16),
            pltpu.VMEM(base_weight.shape, BF16),
            pltpu.VMEM((64, 128), BF16),
            pltpu.VMEM((4, 4, 2, 2, 64, 128), BF16),
            pltpu.VMEM((2, 2, 64, 256), BF16),
            pltpu.VMEM((2, 128, 512), BF16),
            pltpu.VMEM((4, 2, 2, 2, 256, 256), BF16),
            pltpu.VMEM((4, 2, 256, 256), BF16),
            pltpu.VMEM((2, 256, 256), F32),
            pltpu.VMEM((2, 3, 256, 256), BF16),
            pltpu.VMEM((4, 8, 64, 256), BF16),
            pltpu.VMEM((8, 64, 256), F32),
            pltpu.VMEM((8, 3, 64, 256), BF16),
            pltpu.VMEM((8, 4, 16, 512), BF16),
            pltpu.VMEM((32, 16, 512), BF16),
            dma((2,)),
            dma((4, 2)),
            dma((4, 2)),
            dma((4, 2)),
            dma((3,)),
            dma(()),
            dma(()),
            dma(()),
            dma(()),
            dma((4, 4)),
            dma(()),
            dma(()),
            dma(()),
            dma((8,)),
            dma(()),
            dma((32,)),
            pltpu.SemaphoreType.REGULAR((2,)),
        ],
        compiler_params=pltpu.CompilerParams(collective_id=0, has_side_effects=True, vmem_limit_bytes=67043328),
    )(fisher, factor_left, factor_right, base_weight)


def solution(mesh):
    placed = (
        P("lang", None, "blk"),
        P("lang", "blk", None),
        P("lang", None, "blk"),
        P(("lang", "blk"), None),
    )
    return jax.shard_map(
        shards, mesh=mesh, in_specs=placed, out_specs=P(("lang", "blk"), None), check_vma=False
    )
```

time: 476 us -> 52.1 us (0.11)
  waiting for transfers between devices: 355 us -> 0 us
  blocking collectives: 71 us -> 0 us
  Pallas kernels: 0 us -> 49.9 us
  between operations: 14.9 us -> 0.01 us
  starting transfers between devices: 13 us -> 0 us
  local copies, waits for them, and re-layouts: 9.77 us -> 1.87 us
  other arithmetic: 6 us -> 0 us
    all_gather x1 -> x0, waiting for transfers between devices: 208 us -> none  [shards(): lax.all_gather(factor_left, 'blk', axis=1, tiled=True)]
    all_to_all x1 -> x0, waiting for transfers between devices: 93.8 us -> none  [shards(): lax.all_to_all(totals, 'blk', split_axis=1, concat_axis=3, tiled=True)]
    all_to_all x1 -> x0, blocking collectives: 71 us -> none  [shards(): lax.all_to_all(weighted, 'blk', split_axis=1, concat_axis=3, tiled=True)]
    reduce_scatter x2 -> x0, waiting for transfers between devices: 53 us -> none  [the longest x1 52.9 us: shards(): lax.psum_scatter(moved[0], 'lang', scatter_dimension=0, tiled=True)]
    pallas_call x0 -> x1, Pallas kernels: none -> 49.9 us  [shards(): pl.pallas_call(kernel, out_shape=jax.ShapeDtypeStruct(base_weight.shape,...]
    all_to_all x1 -> x0, starting transfers between devices: 12.9 us -> none  [shards(): lax.all_to_all(totals, 'blk', split_axis=1, concat_axis=3, tiled=True)]
    all_to_all x2 -> x0, local copies, waits for them, and re-layouts: 6.9 us -> none  [the longest x1 4.54 us: shards(): lax.all_to_all(totals, 'blk', split_axis=1, concat_axis=3, tiled=True)]
  transfers between devices with their start and end apart: 4 -> 0, of which waited for: 3 -> 0; matrix products, arithmetic and copies ran while one was open for 2% -> 0% of each run, Pallas kernels for 0% -> 0%
where the time goes in v2:
time: 52.1 us; the launch traced here: 51.8 us
  Pallas kernels  49.9 us (96%)
  local copies, waits for them, and re-layouts  1.87 us (4%)
    pallas_call x1, Pallas kernels, shards(): pl.pallas_call(kernel, out_shape=jax.ShapeDtypeStruct(base_weight.shape,...  49.9 us
    unnamed x1, local copies, waits for them, and re-layouts  1.87 us

profile of v2, /device:TPU:32, one launch (start us, length us, event | category | flops | bytes accessed | tf_op | source)
XLA Modules:
  0.0 51.8 jit_solution(17128324398806934229)
XLA Ops:
  0.0 49.9 %shard_map.46 = bf16[16,16384]{1,0:T(8,128)(2,1)} custom-call(bf16[2,4096,256]{2,1,0:T(8,128)(2,1)} %fisher.1, bf16[2,64,64]{2,1,0:T(8,128)(2,1)} %left_hbm.1, bf16[2,64,256]{2,1,0:T(8,128)(2,1)} %right.1, bf16[16,16384]{1,0:T(8,128)(2,1)} %base_hbm.1), custom_call_target="tpu_custom_call" | custom-call | tf_op jit(solution)/shard_map/pallas_call | solution.py:334
  50.0 1.9 %copy.6 = bf16[16,16384]{1,0:T(8,128)(2,1)} copy(bf16[16,16384]{1,0:T(8,128)(2,1)} %shard_map.46) | data formatting | bytes 1048576

commit v3 on v2

--- a/solution.py
+++ b/solution.py
@@ -80,18 +80,8 @@
     left_in = pltpu.make_async_copy(left_hbm, left, in_sem.at[0])
     left_in.start()
 
-    def ranking(c):
-        near, far = (228, 225, 54, 27), (27, 75, 180, 228)
-
-        def pick(options):
-            return jnp.where(zi < 2, jnp.where(zi == 0, options[0], options[1]), jnp.where(zi == 2, options[2], options[3]))
-
-        return jnp.where(zc == c, pick(near), pick(far))
-
-    rank, rank_other = ranking(core), ranking(other)
-
-    def digit(word, n):
-        return lax.shift_right_logical(word, 2 * n) & 3
+    def quarter(n):
+        return n % 2 * 2 + (z + n // 2) % 2
 
     def rows(xs, c, zq):
         return pl.ds(pl.multiple_of(1024 * (2 * xs + c) + 256 * zq, 256), 256)
@@ -104,7 +94,7 @@
 
     for n in range(4):
         for xs in range(2):
-            f_own(digit(rank, n), xs).start()
+            f_own(quarter(n), xs).start()
     r_local = pltpu.make_async_copy(right, rights.at[core], r_sem.at[0])
     r_local.start()
     base_in = pltpu.make_async_copy(base_hbm, base, in_sem.at[1])
@@ -128,22 +118,22 @@
     def _():
         p_near.start()
 
-    f_swap(digit(rank_other, 0), 0).start()
-    f_swap(digit(rank_other, 0), 1).start()
+    f_swap(quarter(0), 0).start()
+    f_swap(quarter(0), 1).start()
     r_remote = remote(right, rights.at[core], r_sem.at[1], r_sem.at[2], partner)
     r_remote.start()
     for n in range(1, 4):
         for xs in range(2):
-            f_swap(digit(rank_other, n), xs).start()
+            f_swap(quarter(n), xs).start()
 
     def t_copy(g, zb):
-        return remote(t_sent.at[g, zb], t_got.at[zb, (g - x + 4) % 4 - 1], t_send, t_recv, dev(g // 2, core, g % 2, z, y))
+        return remote(t_sent.at[g, zb], t_got.at[zb, (g - x + 4) % 4 - 1], t_send, t_recv.at[zb], dev(g // 2, core, g % 2, z, y))
 
     def w_copy(g, u):
         return remote(w_sent.at[g, u], w_got.at[u, (g - x + 4) % 4 - 1], w_send, w_recv.at[u], dev(g // 2, core, g % 2, z, y))
 
     def totals(n, carry):
-        zq, xs = digit(rank, n // 2), n % 2
+        zq, xs = quarter(n // 2), n % 2
         f_own(zq, xs).wait()
         pltpu.make_async_copy(fisher.at[:, rows(xs, core, zq), :], fish.at[zq, xs, other], f_recv.at[zq, xs]).wait()
         t = fish[zq, xs, 0, 0].astype(F32) + fish[zq, xs, 0, 1].astype(F32)
@@ -161,28 +151,31 @@
 
         return carry
 
-    def spread(n, carry):
-        to = dev(xh, core, (xl + n // 8) % 2, (z + n) % 8, y)
+    def spread(xs, n):
+        to = dev(xh, core, xs, (z + n) % 8, y)
         remote(lefts.at[zi, y, :, xl], lefts.at[zi, y, :, xl], z_send, l_recv.at[zi, y], to).start()
-        return carry
-
-    lax.fori_loop(0, 2, totals, 0)
+
     pl.semaphore_wait(token.at[0], 2)
     signal(token.at[1], beside)
 
     @pl.when(home)
     def _():
         pltpu.make_async_copy(lefts.at[zi, y, :, xl], lefts.at[zi, y, :, xl], p_recv).wait()
-        lax.fori_loop(1, 8, spread, 0)
-
-    lax.fori_loop(2, 4, totals, 0)
+        for n in (2, 6, 4):
+            spread(xl, n)
+
+    lax.fori_loop(0, 2, totals, 0)
     pl.semaphore_wait(token.at[1], 1)
 
     @pl.when(home)
     def _():
-        lax.fori_loop(8, 16, spread, 0)
-
-    lax.fori_loop(4, 8, totals, 0)
+        for n in (0, 2, 6, 4):
+            spread(1 - xl, n)
+        for n in (1, 7, 3, 5):
+            spread(xl, n)
+            spread(1 - xl, n)
+
+    lax.fori_loop(2, 8, totals, 0)
     r_local.wait()
     r_remote.wait_recv()
     for s in range(2):
@@ -195,12 +188,8 @@
     def offset(k):
         return ((k + 1) % 3 + 1) * ((k + 2) // 3)
 
-    def first_zb(ys):
-        ahead = (ys - z + 8) % 8
-        return jnp.where((ahead >= 2) & (ahead <= 5), 0, 1)
-
     def forward(n, carry):
-        zq = n % 2 * 2 + (first_zb(y) + n // 2) % 2
+        zq = quarter(n)
         mine = home & (zq == zi)
 
         @pl.when(mine)
@@ -213,19 +202,35 @@
 
         pass_y(zq, 1).start()
         pass_y(zq, 3).start()
-        pass_y(zq, 2).start()
         return carry
 
     lax.fori_loop(0, 4, forward, 0)
+
+    def arrived(zq, ys):
+        pltpu.make_async_copy(lefts.at[zq, ys], lefts.at[zq, ys], l_recv.at[zq, ys]).wait()
+
+    def relay(zq, k):
+        half = lefts.at[zq, (y + offset(k)) % 4, k - 1]
+        remote(half, half, y_send, l_recv.at[zq, (y + offset(k)) % 4], in_y(2 * k - 1)).start()
+
+    def relay_rest(n, carry):
+        zq, k = quarter(2 + n % 2), 1 + n // 2
+        arrived(zq, (y + offset(k)) % 4)
+        relay(zq, k)
+        return carry
 
     def item(n, carry):
         k = n // 2 % 4
+        zq = n % 2 * 2 + (z + n // 8) % 2
         ys = (y + offset(k)) % 4
-        zq = n % 2 * 2 + (first_zb(ys) + n // 8) % 2
-
-        @pl.when(k > 0)
-        def _():
-            pltpu.make_async_copy(lefts.at[zq, ys], lefts.at[zq, ys], l_recv.at[zq, ys]).wait()
+
+        @pl.when((k == 3) | ((k > 0) & (n < 8)))
+        def _():
+            arrived(zq, ys)
+
+        @pl.when(((k == 1) | (k == 2)) & (n < 8))
+        def _():
+            relay(zq, k)
 
         at = pl.ds(pl.multiple_of(ys * 64, 64), 64)
         u = (zq % 2) * 4 + ys
@@ -253,12 +258,12 @@
 
     def combine(step, carry):
         ys = (y + offset(step % 4)) % 4
-        zb = (first_zb(ys) + step // 4) % 2
+        zb = (z + step // 4) % 2
         u = zb * 4 + ys
 
-        @pl.when(step == 0)
-        def _():
-            pltpu.make_async_copy(t_got, t_got, t_recv).wait()
+        @pl.when(step % 4 == 0)
+        def _():
+            pltpu.make_async_copy(t_got.at[zb], t_got.at[zb], t_recv.at[zb]).wait()
 
         pltpu.make_async_copy(w_got.at[u], w_got.at[u], w_recv.at[u]).wait()
         at = pl.ds(pl.multiple_of(ys * 64, 64), 64)
@@ -286,7 +291,7 @@
         return carry
 
     def finish(n, carry):
-        zs = (z + 3 + n % 4 + 4 * (n // 16)) % 8
+        zs = 2 * ((n + z // 2) % 4) + (zc + n // 16) % 2
         src = zs * 4 + (zi - offset(n // 4 % 4) + 4) % 4
         pltpu.make_async_copy(delta_out.at[0, 0], delta_in.at[src], d_recv.at[src]).wait()
         for part, half in ((0, xl), (1, 1 - xl)):
@@ -299,6 +304,10 @@
         @pl.when(m < 8)
         def _():
             lax.fori_loop(2 * m, 2 * m + 2, item, 0)
+
+        @pl.when(m == 3)
+        def _():
+            lax.fori_loop(0, 4, relay_rest, 0)
 
         @pl.when(m >= LAG)
         def _():
@@ -363,15 +372,15 @@
             dma(()),
             dma((4, 4)),
             dma(()),
-            dma(()),
+            dma((2,)),
             dma(()),
             dma((8,)),
             dma(()),
             dma((32,)),
             pltpu.SemaphoreType.REGULAR((2,)),
         ],
-        compiler_params=pltpu.CompilerParams(collective_id=0, has_side_effects=True, vmem_limit_bytes=67043328),
-    )(fisher, factor_left, factor_right, base_weight)
+        compiler_params=pltpu.CompilerParams(collective_id=0, has_side_effects=True, vmem_limit_bytes=50331648),
+    )(*(pltpu.with_memory_space_constraint(a, pltpu.HBM) for a in (fisher, factor_left, factor_right, base_weight)))
 
 
 def solution(mesh):

time: 52.1 us -> 47.9 us (0.919)
  Pallas kernels: 49.9 us -> 47 us
  local copies, waits for them, and re-layouts: 1.87 us -> 0.8 us
    pallas_call x1, Pallas kernels: 49.9 us -> 47 us  [shards(): pl.pallas_call(kernel, out_shape=jax.ShapeDtypeStruct(base_weight.shape,...]
    unnamed x1, local copies, waits for them, and re-layouts: 1.87 us -> 0.8 us
where the time goes in v3:
time: 47.9 us; the launch traced here: 47.8 us
  Pallas kernels  47 us (98%)
  local copies, waits for them, and re-layouts  0.8 us (2%)
    pallas_call x1, Pallas kernels, shards(): pl.pallas_call(kernel, out_shape=jax.ShapeDtypeStruct(base_weight.shape,...  47 us

profile of v3, /device:TPU:32, one launch (start us, length us, event | category | flops | bytes accessed | tf_op | source)
XLA Modules:
  0.0 47.8 jit_solution(16865070215162949661)
XLA Ops:
  0.0 47.0 %shard_map.46 = bf16[16,16384]{1,0:T(8,128)(2,1)S(1)} custom-call(bf16[2,4096,256]{2,1,0:T(8,128)(2,1)} %fisher.1, bf16[2,64,64]{2,1,0:T(8,128)(2,1)} %left_hbm.1, bf16[2,64,256]{2,1,0:T(8,128)(2,1)} %right.1, bf16[16,16384]{1,0:T(8,128)(2,1)} %base_hbm.1), custom_call_target="tpu_custom_call" | custom-call | tf_op jit(solution)/shard_map/pallas_call | solution.py:343
  47.0 0.8 %copy.6 = bf16[16,16384]{1,0:T(8,128)(2,1)} copy(bf16[16,16384]{1,0:T(8,128)(2,1)S(1)} %shard_map.46) | data formatting | bytes 1048576

commit v4 on v3

--- a/solution.py
+++ b/solution.py
@@ -72,13 +72,13 @@
         return dev(xh, core, xl, z, (y + n) % 4)
 
     partner, beside = dev(xh, other, xl, z, y), dev(xh, core, 1 - xl, z, y)
+    left_in = pltpu.make_async_copy(left_hbm, left, in_sem.at[0])
+    left_in.start()
     barrier = pltpu.get_barrier_semaphore()
     for device in (in_z(2), in_z(6), in_y(2), in_z(1), in_z(7), in_y(1), in_y(3), dev(1 - xh, core, xl, z, y),
                    dev(1 - xh, core, 1 - xl, z, y), beside, partner):
         signal(barrier, device)
 
-    left_in = pltpu.make_async_copy(left_hbm, left, in_sem.at[0])
-    left_in.start()
 
     def quarter(n):
         return n % 2 * 2 + (z + n // 2) % 2
@@ -100,9 +100,10 @@
     base_in = pltpu.make_async_copy(base_hbm, base, in_sem.at[1])
     base_in.start()
     weights[...] = jnp.zeros_like(weights)
+    pl.semaphore_wait(barrier, 11)
+    f_swap(quarter(0), 0).start()
     left_in.wait()
     packed[...] = jnp.concatenate([left[0], left[1]], axis=1)
-    pl.semaphore_wait(barrier, 11)
 
     signal(token.at[0], in_z(2))
     signal(token.at[0], in_z(6))
@@ -118,7 +119,6 @@
     def _():
         p_near.start()
 
-    f_swap(quarter(0), 0).start()
     f_swap(quarter(0), 1).start()
     r_remote = remote(right, rights.at[core], r_sem.at[1], r_sem.at[2], partner)
     r_remote.start()
@@ -276,7 +276,8 @@
         for k in range(4):
             delta_out[u, k, :, :256] = near[16 * k : 16 * k + 16]
             delta_out[u, k, :, 256:] = far[16 * k : 16 * k + 16]
-        for k in range(4):
+        for n in (2, 1, 3, 0):
+            k = (y + n) % 4
             here = jnp.logical_and(u == z, k == y)
             d_copy = remote(delta_out.at[u, k], delta_in.at[z * 4 + y], d_send, d_recv.at[z * 4 + y], dev(xh, core, xl, u, k))
 

time: 47.9 us -> 47.9 us (level); the launches traced: 47.8 us -> 47.2 us
  Pallas kernels: 47 us -> 46.4 us
    pallas_call x1, Pallas kernels: 47 us -> 46.4 us  [shards(): pl.pallas_call(kernel, out_shape=jax.ShapeDtypeStruct(base_weight.shape,...]
where the time goes in v4:
time: 47.9 us; the launch traced here: 47.2 us
  Pallas kernels  46.4 us (97%)
  local copies, waits for them, and re-layouts  0.8 us (2%)
    pallas_call x1, Pallas kernels, shards(): pl.pallas_call(kernel, out_shape=jax.ShapeDtypeStruct(base_weight.shape,...  46.4 us

profile of v4, /device:TPU:32, one launch (start us, length us, event | category | flops | bytes accessed | tf_op | source)
XLA Modules:
  0.0 47.2 jit_solution(2339354879534245771)
XLA Ops:
  0.0 46.4 %shard_map.46 = bf16[16,16384]{1,0:T(8,128)(2,1)S(1)} custom-call(bf16[2,4096,256]{2,1,0:T(8,128)(2,1)} %fisher.1, bf16[2,64,64]{2,1,0:T(8,128)(2,1)} %left_hbm.1, bf16[2,64,256]{2,1,0:T(8,128)(2,1)} %right.1, bf16[16,16384]{1,0:T(8,128)(2,1)} %base_hbm.1), custom_call_target="tpu_custom_call" | custom-call | tf_op jit(solution)/shard_map/pallas_call | solution.py:344
  46.4 0.8 %copy.6 = bf16[16,16384]{1,0:T(8,128)(2,1)} copy(bf16[16,16384]{1,0:T(8,128)(2,1)S(1)} %shard_map.46) | data formatting | bytes 1048576

commit v5 on v4

--- a/solution.py
+++ b/solution.py
@@ -8,7 +8,7 @@
 BF16, F32 = jnp.bfloat16, jnp.float32
 NZ, NY = 8, 4
 MESH = pl.DeviceIdType.MESH
-LAG = 3
+LAG = 4
 W_KNEE, W_SCALE = 0.25, 2.0**-7.25
 D_KNEE, D_SCALE = 0.01, 2.0**-7.4
 

time: 47.9 us -> 48.1 us (level)
  Pallas kernels: 46.4 us -> 46.9 us
where the time goes in v5:
time: 48.1 us; the launch traced here: 47.7 us
  Pallas kernels  46.9 us (98%)
  local copies, waits for them, and re-layouts  0.8 us (2%)
    pallas_call x1, Pallas kernels, shards(): pl.pallas_call(kernel, out_shape=jax.ShapeDtypeStruct(base_weight.shape,...  46.9 us

profile of v5, /device:TPU:32, one launch (start us, length us, event | category | flops | bytes accessed | tf_op | source)
XLA Modules:
  0.0 47.7 jit_solution(1494116518904600926)
XLA Ops:
  0.0 46.9 %shard_map.46 = bf16[16,16384]{1,0:T(8,128)(2,1)S(1)} custom-call(bf16[2,4096,256]{2,1,0:T(8,128)(2,1)} %fisher.1, bf16[2,64,64]{2,1,0:T(8,128)(2,1)} %left_hbm.1, bf16[2,64,256]{2,1,0:T(8,128)(2,1)} %right.1, bf16[16,16384]{1,0:T(8,128)(2,1)} %base_hbm.1), custom_call_target="tpu_custom_call" | custom-call | tf_op jit(solution)/shard_map/pallas_call | solution.py:344
  46.9 0.8 %copy.6 = bf16[16,16384]{1,0:T(8,128)(2,1)} copy(bf16[16,16384]{1,0:T(8,128)(2,1)S(1)} %shard_map.46) | data formatting | bytes 1048576
